TPU v7x, 512 devices: a whole 4x4x16 slice. The times are simulated.
512 devices in a mesh: tm: 32 (over z, core), col: 16 (over y, x).
Axes of the slice: x: 4, y: 4, z: 16, core: 2. Of those that a mesh axis runs over, the one named last changes fastest.
Arguments:
- diag_blocks: float32 [64, 768, 768], P('tm', 'col'), may hold values from -0.5 to 2, as said below
- left_blocks: float32 [32, 768, 768], P('tm', 'col'), may hold values from -1 to 0.5
- right_blocks: float32 [32, 768, 768], P('tm', 'col'), may hold values from -1 to 0.5
Outputs:
- blocks: float32 [64, 768, 768], P('tm', 'col')
- solved: float32 [32, 2, 768, 768], P('tm', None, 'col')
Inputs may be any that keep to these rules, and one draw needn't show every extreme that they name: `diag_blocks`: every block is symmetric, and together with left_blocks, right_blocks and their transposes it forms a symmetric positive definite matrix.
All inputs are finite; a program needn't handle non-finite values.
Results may differ from a plain program's by a relative error of at most 0.00013.
Values sent between devices are 32-bit elements; how exact they have to be, the bound alone decides.
A program may use at most 64 MiB of HBM per device.

v0:
```python
import jax
import jax.numpy as jnp
from jax import lax
from jax.sharding import PartitionSpec as P


def passed_along(x, axis, by):
    peers = lax.axis_size(axis)
    return lax.ppermute(x, axis, [(i, (i + by) % peers) for i in range(peers)])


def extended(x, sides, width):
    for axis, dim in sides:
        peers, length = (lax.axis_size(axis), x.shape[dim])
        up = [(i, (i + 1) % peers) for i in range(peers)]
        down = [(j, i) for i, j in up]
        last = lax.slice_in_dim(x, length - width, length, axis=dim)
        first = lax.slice_in_dim(x, 0, width, axis=dim)
        before = lax.ppermute(last, axis, up)
        after = lax.ppermute(first, axis, down)
        x = jnp.concatenate([before, x, after], axis=dim)
    return x


def rows_dot(row_part, full_part):
    return lax.dot_general(
        row_part,
        full_part,
        (((1,), (1,)), ((), ())),
        precision=lax.Precision.HIGHEST,
        preferred_element_type=jnp.float32,
    )


def right_solve(factor, target):
    return lax.linalg.triangular_solve(
        factor, target, left_side=False, lower=True, transpose_a=True
    )


def eliminate(pivot_rows, left_rows, right_rows):
    height = pivot_rows.shape[0]
    row_start = lax.axis_index("col") * height
    pivot_full = lax.all_gather(pivot_rows, "col", axis=0, tiled=True)
    factor = jnp.linalg.cholesky(pivot_full)
    solved_left = right_solve(factor, left_rows)
    solved_right = right_solve(factor, right_rows)
    full_left, full_right = (
        lax.all_gather(solved_left, "col", axis=0, tiled=True),
        lax.all_gather(solved_right, "col", axis=0, tiled=True),
    )
    factor_rows = lax.dynamic_slice_in_dim(factor, row_start, height, 0)
    return (
        factor_rows,
        solved_left,
        solved_right,
        full_left,
        full_right,
        solved_left,
        solved_right,
    )


def shards(diag_blocks, left_blocks, right_blocks):
    even_rows = diag_blocks[0]
    odd_rows = diag_blocks[1]
    factor_one, solved_left, solved_right, full_left, full_right, back_left, back_right = eliminate(
        odd_rows, left_blocks[0], right_blocks[0]
    )
    left_gram = rows_dot(back_left, full_left)
    right_gram = rows_dot(back_right, full_right)
    upper_rows = -rows_dot(back_left, full_right)
    mirror_upper = -rows_dot(back_right, full_left)
    right_prev, mirror_lower = passed_along((right_gram, upper_rows), "tm", 1)
    reduced = even_rows - left_gram - right_prev
    factor_two, first_solved, second_solved, first_full, second_full, first_back, second_back = (
        eliminate(reduced, mirror_lower, mirror_upper)
    )
    second_grams = jnp.stack([rows_dot(first_back, first_full), rows_dot(second_back, second_full)])
    halo_rows = extended(second_grams, (("tm", 0),), 1)
    final_block = reduced - halo_rows[3] - halo_rows[0]
    blocks = jnp.stack([final_block, factor_one])
    solved = jnp.stack([solved_left, solved_right])[None]
    return (blocks, solved)


def solution(mesh):
    in_specs = (P("tm", "col", None), P("tm", "col", None), P("tm", "col", None))
    out_specs = (P("tm", "col", None), P("tm", None, "col", None))
    return jax.shard_map(shards, mesh=mesh, in_specs=in_specs, out_specs=out_specs, check_vma=False)
```

profile of v0, /device:TPU:1, one launch (start us, length us, event | category | flops | bytes accessed | tf_op | source)
XLA Modules:
  0.0 874.4 jit_solution(16462688095010835249)
XLA Ops:
  9.0 67.3 %all-gather.18.cloned.1.call-done = f32[1,768,768]{2,0,1:T(1,128)} async-done(((f32[1,48,768]{2,0,1:T(1,128)}), f32[1,768,768]{2,0,1:T(1,128)}) %all-gather.18.cloned.1.call-update) | async-done | bytes 2359312 | tf_op jit(solution)/shard_map/all_gather | solution.py:44
  86.6 11.7 %cholesky.453 = f32[128,128]{1,0:T(8,128)S(1)} custom-call(f32[128,128]{1,0:T(8,128)S(1)} %cholesky.669), custom_call_target="Cholesky" | custom-call | tf_op jit(solution)/shard_map/jit(cholesky)/cholesky | solution.py:45
  111.1 11.7 %cholesky.472 = f32[128,128]{1,0:T(8,128)S(1)} custom-call(f32[128,128]{1,0:T(8,128)S(1)} %cholesky.673), custom_call_target="Cholesky" | custom-call | tf_op jit(solution)/shard_map/jit(cholesky)/cholesky | solution.py:45
  122.8 10.0 %custom-call.44 = f32[1,128,128]{1,2,0:T(8,128)S(1)} custom-call(f32[1,128,128]{2,1,0:T(8,128)S(1)} %get-tuple-element.86), custom_call_target="InvertDiagBlocksLowerTriangular" | custom-call | tf_op jit(solution)/shard_map/jit(cholesky)/cholesky | solution.py:45
  134.7 11.7 %cholesky.493 = f32[128,128]{1,0:T(8,128)S(1)} custom-call(f32[128,128]{1,0:T(8,128)S(1)} %cholesky.678), custom_call_target="Cholesky" | custom-call | tf_op jit(solution)/shard_map/jit(cholesky)/cholesky | solution.py:45
  158.8 12.1 %cholesky.512 = f32[128,128]{1,0:T(8,128)S(1)} custom-call(f32[128,128]{1,0:T(8,128)S(1)} %cholesky.683), custom_call_target="Cholesky" | custom-call | tf_op jit(solution)/shard_map/jit(cholesky)/cholesky | solution.py:45
  183.2 11.7 %cholesky.531 = f32[128,128]{1,0:T(8,128)S(1)} custom-call(f32[128,128]{1,0:T(8,128)S(1)} %cholesky.688), custom_call_target="Cholesky" | custom-call | tf_op jit(solution)/shard_map/jit(cholesky)/cholesky | solution.py:45
  207.0 11.9 %cholesky.548 = f32[128,128]{1,0:T(8,128)S(1)} custom-call(f32[128,128]{1,0:T(8,128)S(1)} %convolution_subtract_fusion.5), custom_call_target="Cholesky" | custom-call | tf_op jit(solution)/shard_map/jit(cholesky)/cholesky | solution.py:45
  226.6 17.4 %while.8 = (s32[]{:T(128)}, f32[768,768]{1,0:T(8,128)}, s32[6,2]{0,1:T(2,128)S(1)}, f32[6,128,128]{2,1,0:T(8,128)S(1)}, s32[]{:T(128)}) while((s32[]{:T(128)}, f32[768,768]{1,0:T(8,128)}, s32[6,2]{0,1:T(2,128)S(1)}, f32[6,128,128]{2,1,0:T(8,128)S(1)}, s32[]{:T(128)}) %tuple.107), condition=%wide.while_cond, body=%wide.while_body.sunk | while | flops 2 | bytes 131189 | solution.py:36
  243.9 59.0 %custom-call.48 = f32[6,128,128]{1,2,0:T(8,128)S(1)} custom-call(f32[6,128,128]{2,1,0:T(8,128)S(1)} %get-tuple-element.30), custom_call_target="InvertDiagBlocksLowerTriangular" | custom-call | tf_op jit(solution)/shard_map/triangular_solve/custom-call.5 | solution.py:36
  319.3 52.2 %all-gather.10.cloned.1.call-done = f32[768,768]{1,0:T(8,128)} async-done(((f32[48,768]{1,0:T(8,128)}), f32[768,768]{1,0:T(8,128)}) %all-gather.10.cloned.1.call-update) | async-done | bytes 2359312 | tf_op jit(solution)/shard_map/all_gather | solution.py:50
  378.6 56.7 %all-gather.8.cloned.1.call-done = f32[768,768]{1,0:T(8,128)} async-done(((f32[48,768]{1,0:T(8,128)}), f32[768,768]{1,0:T(8,128)}) %all-gather.8.cloned.1.call-update) | async-done | bytes 2359312 | tf_op jit(solution)/shard_map/all_gather | solution.py:49
  442.4 58.0 %all-gather.12.cloned.1.call-done = f32[768,768]{1,0:T(8,128)} async-done(((f32[48,768]{1,0:T(8,128)}), f32[768,768]{1,0:T(8,128)}) %all-gather.12.cloned.1.call-update) | async-done | bytes 2359312 | tf_op jit(solution)/shard_map/all_gather | solution.py:44
  507.5 11.7 %cholesky.563 = f32[128,128]{1,0:T(8,128)S(1)} custom-call(f32[128,128]{1,0:T(8,128)S(1)} %cholesky.692), custom_call_target="Cholesky" | custom-call | tf_op jit(solution)/shard_map/jit(cholesky)/cholesky | solution.py:45
  532.7 11.7 %cholesky.582 = f32[128,128]{1,0:T(8,128)S(1)} custom-call(f32[128,128]{1,0:T(8,128)S(1)} %cholesky.696), custom_call_target="Cholesky" | custom-call | tf_op jit(solution)/shard_map/jit(cholesky)/cholesky | solution.py:45
  545.1 9.9 %custom-call.51 = f32[1,128,128]{1,2,0:T(8,128)S(1)} custom-call(f32[1,128,128]{2,1,0:T(8,128)S(1)} %get-tuple-element.70), custom_call_target="InvertDiagBlocksLowerTriangular" | custom-call | tf_op jit(solution)/shard_map/jit(cholesky)/cholesky | solution.py:45
  557.0 11.7 %cholesky.603 = f32[128,128]{1,0:T(8,128)S(1)} custom-call(f32[128,128]{1,0:T(8,128)S(1)} %cholesky.701), custom_call_target="Cholesky" | custom-call | tf_op jit(solution)/shard_map/jit(cholesky)/cholesky | solution.py:45
  581.1 11.9 %cholesky.622 = f32[128,128]{1,0:T(8,128)S(1)} custom-call(f32[128,128]{1,0:T(8,128)S(1)} %cholesky.706), custom_call_target="Cholesky" | custom-call | tf_op jit(solution)/shard_map/jit(cholesky)/cholesky | solution.py:45
  605.4 11.7 %cholesky.641 = f32[128,128]{1,0:T(8,128)S(1)} custom-call(f32[128,128]{1,0:T(8,128)S(1)} %cholesky.711), custom_call_target="Cholesky" | custom-call | tf_op jit(solution)/shard_map/jit(cholesky)/cholesky | solution.py:45
  629.1 12.1 %cholesky.658 = f32[128,128]{1,0:T(8,128)S(1)} custom-call(f32[128,128]{1,0:T(8,128)S(1)} %slice_subtract_fusion.4), custom_call_target="Cholesky" | custom-call | tf_op jit(solution)/shard_map/jit(cholesky)/cholesky | solution.py:45
  647.2 17.3 %while.9 = (s32[]{:T(128)}, f32[768,768]{1,0:T(8,128)}, s32[6,2]{0,1:T(2,128)S(1)}, f32[6,128,128]{2,1,0:T(8,128)S(1)}, s32[]{:T(128)}) while((s32[]{:T(128)}, f32[768,768]{1,0:T(8,128)}, s32[6,2]{0,1:T(2,128)S(1)}, f32[6,128,128]{2,1,0:T(8,128)S(1)}, s32[]{:T(128)}) %tuple.125), condition=%wide.while_cond.clone.1, body=%wide.while_body.clone.1.sunk | while | flops 2 | bytes 131189 | solution.py:36
  665.2 59.8 %custom-call.55 = f32[6,128,128]{1,2,0:T(8,128)S(1)} custom-call(f32[6,128,128]{2,1,0:T(8,128)} %copy-done.15), custom_call_target="InvertDiagBlocksLowerTriangular" | custom-call | tf_op jit(solution)/shard_map/triangular_solve/custom-call.5 | solution.py:36
  749.1 44.4 %all-gather.16.cloned.1.call-done = f32[768,768]{1,0:T(8,128)} async-done(((f32[48,768]{1,0:T(8,128)}), f32[768,768]{1,0:T(8,128)}) %all-gather.16.cloned.1.call-update) | async-done | bytes 2359312 | tf_op jit(solution)/shard_map/all_gather | solution.py:50
  800.6 55.9 %all-gather.14.cloned.1.call-done = f32[768,768]{1,0:T(8,128)} async-done(((f32[48,768]{1,0:T(8,128)}), f32[768,768]{1,0:T(8,128)}) %all-gather.14.cloned.1.call-update) | async-done | bytes 2359312 | tf_op jit(solution)/shard_map/all_gather | solution.py:49
  (223 shorter events, 236.7 us)
Async XLA Ops:
  7.2 69.1 %all-gather.18.cloned.1.call-start = ((), (), s32[]{:S(2)}) async-start(), calls=%async_computation.5 | async-start | bytes 2506752 | tf_op jit(solution)/shard_map/all_gather | solution.py:44
  9.0 362.5 %all-gather.10.cloned.1.call-start = ((), (), s32[]{:S(2)}) async-start(), calls=%async_computation.1 | async-start | bytes 2506752 | tf_op jit(solution)/shard_map/all_gather | solution.py:50
  76.3 6.9 copy-start
  85.1 1.4 copy-start.5
  224.1 78.9 %copy-start.17 = (f32[1,48,768]{2,1,0:T(8,128)S(1)}, f32[1,48,768]{2,1,0:T(8,128)}, u32[]{:S(2)}) copy-start(f32[1,48,768]{2,1,0:T(8,128)} %param.8) | copy-start | bytes 442372
  226.5 84.6 %copy-start.18 = (f32[1,48,768]{2,1,0:T(8,128)S(1)}, f32[1,48,768]{2,1,0:T(8,128)}, u32[]{:S(2)}) copy-start(f32[1,48,768]{2,1,0:T(8,128)} %param.7) | copy-start | bytes 442372
  311.0 60.4 %copy-start.9 = (f32[48,768]{1,0:T(8,128)S(1)}, f32[48,768]{1,0:T(8,128)}, u32[]{:S(2)}) copy-start(f32[48,768]{1,0:T(8,128)} %copy-done.8) | copy-start | bytes 442372
  311.0 124.2 %all-gather.8.cloned.1.call-start = ((), (), s32[]{:S(2)}) async-start(), calls=%async_computation | async-start | bytes 2506752 | tf_op jit(solution)/shard_map/all_gather | solution.py:49
  313.7 121.6 %copy-start.16 = (f32[2,48,768]{2,1,0:T(8,128)S(1)}, f32[2,48,768]{2,1,0:T(8,128)}, u32[]{:S(2)}) copy-start(f32[2,48,768]{2,1,0:T(8,128)} %param.6) | copy-start | bytes 884740
  319.2 116.1 %copy-start.7 = (f32[48,768]{1,0:T(8,128)S(1)}, f32[48,768]{1,0:T(8,128)}, u32[]{:S(2)}) copy-start(f32[48,768]{1,0:T(8,128)} %copy-done.6) | copy-start | bytes 442372
  319.2 181.2 %all-gather.12.cloned.1.call-start = ((), (), s32[]{:S(2)}) async-start(), calls=%async_computation.2 | async-start | bytes 2506752 | tf_op jit(solution)/shard_map/all_gather | solution.py:44
  375.4 59.9 %collective-permute-start = (f32[48,768]{1,0:T(8,128)S(1)}, f32[48,768]{1,0:T(8,128)S(1)}, u32[]{:S(2)}, u32[]{:S(2)}) collective-permute-start(f32[48,768]{1,0:T(8,128)S(1)} %fusion.179), channel_id=1, source_target_pairs={{0,16},{16,32},{32,48},{48,64},{64,80},{80,96},{96,112},{112,128},... | collective-permute-start | bytes 442376 | tf_op jit(solution)/shard_map/ppermute | solution.py:9
  435.3 4.8 copy-start.3
  440.1 353.4 %all-gather.16.cloned.1.call-start = ((), (), s32[]{:S(2)}) async-start(), calls=%async_computation.4 | async-start | bytes 2506752 | tf_op jit(solution)/shard_map/all_gather | solution.py:50
  500.4 3.7 copy-start.1
  506.1 1.4 copy-start.4
  647.2 86.2 %copy-start.2 = (f32[768,768]{1,0:T(8,128)S(1)}, f32[768,768]{1,0:T(8,128)}, u32[]{:S(2)}) copy-start(f32[768,768]{1,0:T(8,128)} %all-gather.10.cloned.1.call-done) | copy-start | bytes 7077892
  733.1 60.4 %copy-start.12 = (f32[48,768]{1,0:T(8,128)S(1)}, f32[48,768]{1,0:T(8,128)}, u32[]{:S(2)}) copy-start(f32[48,768]{1,0:T(8,128)} %copy-done.11) | copy-start | bytes 442372
  733.1 123.5 %all-gather.14.cloned.1.call-start = ((), (), s32[]{:S(2)}) async-start(), calls=%async_computation.3 | async-start | bytes 2506752 | tf_op jit(solution)/shard_map/all_gather | solution.py:49
  735.6 5.3 collective-permute-start.1
  749.0 107.5 %copy-start.14 = (f32[48,768]{1,0:T(8,128)S(1)}, f32[48,768]{1,0:T(8,128)}, u32[]{:S(2)}) copy-start(f32[48,768]{1,0:T(8,128)} %copy-done.13) | copy-start | bytes 442372
  797.4 69.2 %copy-start.10 = (f32[48,768]{1,0:T(8,128)S(1)}, f32[48,768]{1,0:T(8,128)}, u32[]{:S(2)}) copy-start(f32[48,768]{1,0:T(8,128)} %fusion.4) | copy-start | bytes 442372
  797.4 66.8 %collective-permute-start.3 = (f32[1,48,768]{2,1,0:T(8,128)S(1)}, f32[1,48,768]{2,1,0:T(8,128)S(1)}, u32[]{:S(2)}, u32[]{:S(2)}) collective-permute-start(f32[1,48,768]{2,1,0:T(8,128)S(1)} %convolution_bitcast_fusion), channel_id=1, source_target_pairs={{0,16},{16,32},{32,48},{48,64},{64,80},{80,96},{96,112},{112,128},... | collective-permute-start | bytes 442376 | tf_op jit(solution)/shard_map/ppermute | solution.py:19
  860.5 6.1 collective-permute-start.2
  (5 other events, 3.4 us)
Sparse Core Ops, SparseCore 0:
  11.6 64.6 all-gather.17
  311.1 60.2 all-gather.9
  375.0 60.1 all-gather.7
  440.2 60.1 all-gather.11
  733.2 60.2 all-gather.15
  796.3 60.1 all-gather.13
where the time goes:
time: 885 us; the launch traced here: 874 us
  other arithmetic  376 us (42%)
  waiting for transfers between devices  339 us (38%)
  matrix products  70.1 us (8%)
  local copies, waits for them, and re-layouts  54.3 us (6%)
  between operations  22.7 us (3%)
  starting transfers between devices  12.2 us (1%)
    another operation x45, other arithmetic, eliminate(): factor = jnp.linalg.cholesky(pivot_full)  248 us
    all_gather x2, waiting for transfers between devices, eliminate(): pivot_full = lax.all_gather(pivot_rows, 'col', axis=0, tiled=True)  125 us
    another operation x5, other arithmetic, right_solve(): lax.linalg.triangular_solve(factor, target, left_side=False, lower=True,...  123 us
    all_gather x2, waiting for transfers between devices, eliminate(): lax.all_gather(solved_left, 'col', axis=0, tiled=True)  113 us
    all_gather x2, waiting for transfers between devices, eliminate(): lax.all_gather(solved_right, 'col', axis=0, tiled=True)  96.6 us
    another operation x39, local copies, waits for them, and re-layouts, right_solve(): lax.linalg.triangular_solve(factor, target, left_side=False, lower=True,...  34.5 us
    another operation x44, matrix products, right_solve(): lax.linalg.triangular_solve(factor, target, left_side=False, lower=True,...  29.3 us
    dot_general x6, matrix products, rows_dot(): lax.dot_general(row_part, full_part, (((1,), (1,)), ((), ())), precision=...  21.1 us
  transfers between devices with their start and end apart: 10, of which 8 were waited for; matrix products, arithmetic and copies ran while one was open for 4% of the time, Pallas kernels for 0%

commit v1 on v0

--- a/solution.py
+++ b/solution.py
@@ -2,6 +2,11 @@
 import jax.numpy as jnp
 from jax import lax
 from jax.sharding import PartitionSpec as P
+
+
+def swapped_in(array, mesh_axis, dim):
+    stack = jnp.stack([array] * lax.axis_size(mesh_axis))
+    return jnp.concatenate(lax.all_to_all(stack, mesh_axis, 0, 0), axis=dim)
 
 
 def passed_along(x, axis, by):
@@ -46,7 +51,7 @@
     solved_left = right_solve(factor, left_rows)
     solved_right = right_solve(factor, right_rows)
     full_left, full_right = (
-        lax.all_gather(solved_left, "col", axis=0, tiled=True),
+        swapped_in(solved_left, "col", 0),
         lax.all_gather(solved_right, "col", axis=0, tiled=True),
     )
     factor_rows = lax.dynamic_slice_in_dim(factor, row_start, height, 0)

time: 885 us -> 807 us (0.912)
  waiting for transfers between devices: 339 us -> 240 us
  starting transfers between devices: 12.2 us -> 23.6 us
  other arithmetic: 376 us -> 386 us
    all_gather x2 -> x0, waiting for transfers between devices: 113 us -> none  [eliminate(): lax.all_gather(solved_left, 'col', axis=0, tiled=True)]
    all_to_all x0 -> x2, waiting for transfers between devices: none -> 30.7 us  [swapped_in(): return jnp.concatenate(lax.all_to_all(stack, mesh_axis, 0, 0), axis=dim)]
    all_gather x2, waiting for transfers between devices: 96.6 us -> 85.3 us  [eliminate(): lax.all_gather(solved_right, 'col', axis=0, tiled=True)]
    another operation x45, other arithmetic: 248 us -> 258 us  [eliminate(): factor = jnp.linalg.cholesky(pivot_full)]
  transfers between devices with their start and end apart: 10 -> 10, of which waited for: 8 -> 7; matrix products, arithmetic and copies ran while one was open for 4% -> 33% of each run, Pallas kernels for 0% -> 0%
where the time goes in v1:
time: 807 us; the launch traced here: 795 us
  other arithmetic  386 us (48%)
  waiting for transfers between devices  240 us (30%)
  matrix products  66.6 us (8%)
  local copies, waits for them, and re-layouts  56.6 us (7%)
  starting transfers between devices  23.6 us (3%)
  between operations  22.6 us (3%)
    another operation x45, other arithmetic, eliminate(): factor = jnp.linalg.cholesky(pivot_full)  258 us
    another operation x5, other arithmetic, right_solve(): lax.linalg.triangular_solve(factor, target, left_side=False, lower=True,...  122 us
    all_gather x2, waiting for transfers between devices, eliminate(): pivot_full = lax.all_gather(pivot_rows, 'col', axis=0, tiled=True)  121 us
    all_gather x2, waiting for transfers between devices, eliminate(): lax.all_gather(solved_right, 'col', axis=0, tiled=True)  85.3 us
    another operation x39, local copies, waits for them, and re-layouts, right_solve(): lax.linalg.triangular_solve(factor, target, left_side=False, lower=True,...  35.1 us
    all_to_all x2, waiting for transfers between devices, swapped_in(): return jnp.concatenate(lax.all_to_all(stack, mesh_axis, 0, 0), axis=dim)  30.7 us
    another operation x44, matrix products, right_solve(): lax.linalg.triangular_solve(factor, target, left_side=False, lower=True,...  29.3 us
    another operation x20, matrix products, eliminate(): factor = jnp.linalg.cholesky(pivot_full)  19.6 us
  transfers between devices with their start and end apart: 10, of which 7 were waited for; matrix products, arithmetic and copies ran while one was open for 33% of the time, Pallas kernels for 0%

profile of v1, /device:TPU:1, one launch (start us, length us, event | category | flops | bytes accessed | tf_op | source)
XLA Modules:
  0.0 795.0 jit_solution(2484614803483796823)
XLA Ops:
  9.0 67.3 %all-gather.12.cloned.1.call-done = f32[1,768,768]{2,0,1:T(1,128)} async-done(((f32[1,48,768]{2,0,1:T(1,128)}), f32[1,768,768]{2,0,1:T(1,128)}) %all-gather.12.cloned.1.call-update) | async-done | bytes 2359312 | tf_op jit(solution)/shard_map/all_gather | solution.py:49
  86.5 11.7 %cholesky.453 = f32[128,128]{1,0:T(8,128)S(1)} custom-call(f32[128,128]{1,0:T(8,128)S(1)} %cholesky.669), custom_call_target="Cholesky" | custom-call | tf_op jit(solution)/shard_map/jit(cholesky)/cholesky | solution.py:50
  98.3 9.8 %custom-call.43 = f32[1,128,128]{1,2,0:T(8,128)S(1)} custom-call(f32[1,128,128]{2,1,0:T(8,128)S(1)} %get-tuple-element.89), custom_call_target="InvertDiagBlocksLowerTriangular" | custom-call | tf_op jit(solution)/shard_map/jit(cholesky)/cholesky | solution.py:50
  111.1 11.7 %cholesky.472 = f32[128,128]{1,0:T(8,128)S(1)} custom-call(f32[128,128]{1,0:T(8,128)S(1)} %cholesky.673), custom_call_target="Cholesky" | custom-call | tf_op jit(solution)/shard_map/jit(cholesky)/cholesky | solution.py:50
  122.8 18.6 %custom-call.44 = f32[1,128,128]{1,2,0:T(8,128)S(1)} custom-call(f32[1,128,128]{2,1,0:T(8,128)S(1)} %get-tuple-element.86), custom_call_target="InvertDiagBlocksLowerTriangular" | custom-call | tf_op jit(solution)/shard_map/jit(cholesky)/cholesky | solution.py:50
  143.3 11.7 %cholesky.493 = f32[128,128]{1,0:T(8,128)S(1)} custom-call(f32[128,128]{1,0:T(8,128)S(1)} %cholesky.678), custom_call_target="Cholesky" | custom-call | tf_op jit(solution)/shard_map/jit(cholesky)/cholesky | solution.py:50
  167.5 12.1 %cholesky.512 = f32[128,128]{1,0:T(8,128)S(1)} custom-call(f32[128,128]{1,0:T(8,128)S(1)} %cholesky.683), custom_call_target="Cholesky" | custom-call | tf_op jit(solution)/shard_map/jit(cholesky)/cholesky | solution.py:50
  191.8 11.7 %cholesky.531 = f32[128,128]{1,0:T(8,128)S(1)} custom-call(f32[128,128]{1,0:T(8,128)S(1)} %cholesky.688), custom_call_target="Cholesky" | custom-call | tf_op jit(solution)/shard_map/jit(cholesky)/cholesky | solution.py:50
  215.6 11.9 %cholesky.548 = f32[128,128]{1,0:T(8,128)S(1)} custom-call(f32[128,128]{1,0:T(8,128)S(1)} %convolution_subtract_fusion.5), custom_call_target="Cholesky" | custom-call | tf_op jit(solution)/shard_map/jit(cholesky)/cholesky | solution.py:50
  235.1 17.4 %while.8 = (s32[]{:T(128)}, f32[768,768]{1,0:T(8,128)}, s32[6,2]{0,1:T(2,128)S(1)}, f32[6,128,128]{2,1,0:T(8,128)S(1)}, s32[]{:T(128)}) while((s32[]{:T(128)}, f32[768,768]{1,0:T(8,128)}, s32[6,2]{0,1:T(2,128)S(1)}, f32[6,128,128]{2,1,0:T(8,128)S(1)}, s32[]{:T(128)}) %tuple.107), condition=%wide.while_cond, body=%wide.while_body.sunk | while | flops 2 | bytes 131189 | solution.py:41
  252.5 59.0 %custom-call.48 = f32[6,128,128]{1,2,0:T(8,128)S(1)} custom-call(f32[6,128,128]{2,1,0:T(8,128)S(1)} %get-tuple-element.30), custom_call_target="InvertDiagBlocksLowerTriangular" | custom-call | tf_op jit(solution)/shard_map/triangular_solve/custom-call.5 | solution.py:41
  332.9 62.2 %all-gather.6.cloned.1.call-done = f32[768,768]{1,0:T(8,128)} async-done(((f32[48,768]{1,0:T(8,128)}), f32[768,768]{1,0:T(8,128)}) %all-gather.6.cloned.1.call-update) | async-done | bytes 2359312 | tf_op jit(solution)/shard_map/all_gather | solution.py:55
  414.5 53.7 %all-gather.8.cloned.1.call-done = f32[768,768]{1,0:T(8,128)} async-done(((f32[48,768]{1,0:T(8,128)}), f32[768,768]{1,0:T(8,128)}) %all-gather.8.cloned.1.call-update) | async-done | bytes 2359312 | tf_op jit(solution)/shard_map/all_gather | solution.py:49
  475.2 11.7 %cholesky.563 = f32[128,128]{1,0:T(8,128)S(1)} custom-call(f32[128,128]{1,0:T(8,128)S(1)} %cholesky.692), custom_call_target="Cholesky" | custom-call | tf_op jit(solution)/shard_map/jit(cholesky)/cholesky | solution.py:50
  501.0 12.5 %cholesky.582 = f32[128,128]{1,0:T(8,128)S(1)} custom-call(f32[128,128]{1,0:T(8,128)} %cholesky.696), custom_call_target="Cholesky" | custom-call | tf_op jit(solution)/shard_map/jit(cholesky)/cholesky | solution.py:50
  514.9 10.8 %custom-call.51 = f32[1,128,128]{1,2,0:T(8,128)S(1)} custom-call(f32[1,128,128]{2,1,0:T(8,128)} %get-tuple-element.70), custom_call_target="InvertDiagBlocksLowerTriangular" | custom-call | tf_op jit(solution)/shard_map/jit(cholesky)/cholesky | solution.py:50
  527.6 11.7 %cholesky.603 = f32[128,128]{1,0:T(8,128)S(1)} custom-call(f32[128,128]{1,0:T(8,128)S(1)} %cholesky.701), custom_call_target="Cholesky" | custom-call | tf_op jit(solution)/shard_map/jit(cholesky)/cholesky | solution.py:50
  551.7 11.9 %cholesky.622 = f32[128,128]{1,0:T(8,128)S(1)} custom-call(f32[128,128]{1,0:T(8,128)S(1)} %cholesky.706), custom_call_target="Cholesky" | custom-call | tf_op jit(solution)/shard_map/jit(cholesky)/cholesky | solution.py:50
  575.9 11.7 %cholesky.641 = f32[128,128]{1,0:T(8,128)S(1)} custom-call(f32[128,128]{1,0:T(8,128)S(1)} %cholesky.711), custom_call_target="Cholesky" | custom-call | tf_op jit(solution)/shard_map/jit(cholesky)/cholesky | solution.py:50
  599.6 12.0 %cholesky.658 = f32[128,128]{1,0:T(8,128)S(1)} custom-call(f32[128,128]{1,0:T(8,128)S(1)} %slice_subtract_fusion.4), custom_call_target="Cholesky" | custom-call | tf_op jit(solution)/shard_map/jit(cholesky)/cholesky | solution.py:50
  617.7 17.9 %while.9 = (s32[]{:T(128)}, f32[768,768]{1,0:T(8,128)}, s32[6,2]{0,1:T(2,128)S(1)}, f32[6,128,128]{2,1,0:T(8,128)S(1)}, s32[]{:T(128)}) while((s32[]{:T(128)}, f32[768,768]{1,0:T(8,128)}, s32[6,2]{0,1:T(2,128)S(1)}, f32[6,128,128]{2,1,0:T(8,128)S(1)}, s32[]{:T(128)}) %tuple.121), condition=%wide.while_cond.clone.1, body=%wide.while_body.clone.1.sunk | while | flops 2 | bytes 131189 | solution.py:41
  635.5 59.0 %custom-call.55 = f32[6,128,128]{1,2,0:T(8,128)S(1)} custom-call(f32[6,128,128]{2,1,0:T(8,128)S(1)} %get-tuple-element.32), custom_call_target="InvertDiagBlocksLowerTriangular" | custom-call | tf_op jit(solution)/shard_map/triangular_solve/custom-call.5 | solution.py:41
  715.7 30.7 %all-to-all-done.1 = f32[16,48,768]{2,1,0:T(8,128)S(1)} async-done(((f32[16,48,768]{2,1,0:T(8,128)}), f32[16,48,768]{2,1,0:T(8,128)S(1)}, u32[]{:S(2)}, u32[]{:S(2)}) %all-to-all-start.1) | async-done | bytes 2359328 | tf_op jit(solution)/shard_map/all_to_all | solution.py:9
  754.9 23.1 %all-gather.10.cloned.1.call-done = f32[768,768]{1,0:T(8,128)} async-done(((f32[48,768]{1,0:T(8,128)}), f32[768,768]{1,0:T(8,128)}) %all-gather.10.cloned.1.call-update) | async-done | bytes 2359312 | tf_op jit(solution)/shard_map/all_gather | solution.py:55
  (211 shorter events, 235.8 us)
Async XLA Ops:
  7.2 69.1 %all-gather.12.cloned.1.call-start = ((), (), s32[]{:S(2)}) async-start(), calls=%async_computation.5 | async-start | bytes 2506752 | tf_op jit(solution)/shard_map/all_gather | solution.py:49
  9.0 386.1 %all-gather.6.cloned.1.call-start = ((), (), s32[]{:S(2)}) async-start(), calls=%async_computation.2 | async-start | bytes 2506752 | tf_op jit(solution)/shard_map/all_gather | solution.py:55
  76.3 6.8 copy-start.1
  85.1 1.4 copy-start.4
  232.6 78.8 %copy-start.11 = (f32[1,48,768]{2,1,0:T(8,128)S(1)}, f32[1,48,768]{2,1,0:T(8,128)}, u32[]{:S(2)}) copy-start(f32[1,48,768]{2,1,0:T(8,128)} %param.8) | copy-start | bytes 442372
  235.0 84.5 %copy-start.12 = (f32[1,48,768]{2,1,0:T(8,128)S(1)}, f32[1,48,768]{2,1,0:T(8,128)}, u32[]{:S(2)}) copy-start(f32[1,48,768]{2,1,0:T(8,128)} %param.7) | copy-start | bytes 442372
  318.9 0.7 copy-start.5
  328.6 66.5 %copy-start.6 = (f32[48,768]{1,0:T(8,128)S(1)}, f32[48,768]{1,0:T(8,128)}, u32[]{:S(2)}) copy-start(f32[48,768]{1,0:T(8,128)} %copy-done.5) | copy-start | bytes 442372
  328.6 73.7 %all-to-all-start = ((f32[16,48,768]{2,1,0:T(8,128)}), f32[16,48,768]{2,1,0:T(8,128)S(1)}, u32[]{:S(2)}, u32[]{:S(2)}) async-start(f32[16,48,768]{2,1,0:T(8,128)} %stack.20), calls=%async_computation | async-start | bytes 4718592 | tf_op jit(solution)/shard_map/all_to_all | solution.py:9
  332.8 71.5 %copy-start.10 = (f32[2,48,768]{2,1,0:T(8,128)S(1)}, f32[2,48,768]{2,1,0:T(8,128)}, u32[]{:S(2)}) copy-start(f32[2,48,768]{2,1,0:T(8,128)} %param.6) | copy-start | bytes 884740
  332.8 135.3 %all-gather.8.cloned.1.call-start = ((), (), s32[]{:S(2)}) async-start(), calls=%async_computation.3 | async-start | bytes 2506752 | tf_op jit(solution)/shard_map/all_gather | solution.py:49
  399.0 5.3 collective-permute-start
  407.4 370.7 %all-gather.10.cloned.1.call-start = ((), (), s32[]{:S(2)}) async-start(), calls=%async_computation.4 | async-start | bytes 2506752 | tf_op jit(solution)/shard_map/all_gather | solution.py:55
  407.4 2.3 copy-start.2
  412.0 290.6 %collective-permute-start.1 = (f32[48,768]{1,0:T(8,128)S(1)}, f32[48,768]{1,0:T(8,128)S(1)}, u32[]{:S(2)}, u32[]{:S(2)}) collective-permute-start(f32[48,768]{1,0:T(8,128)S(1)} %convolution_negate_fusion.1), channel_id=1, source_target_pairs={{0,16},{16,32},{32,48},{48,64},{64,80},{80,96},{96,112},{112,128},... | collective-permute-start | bytes 442376 | tf_op jit(solution)/shard_map/ppermute | solution.py:14
  468.2 3.6 copy-start
  473.8 1.4 copy-start.3
  701.9 0.7 copy-start.8
  711.6 34.8 %all-to-all-start.1 = ((f32[16,48,768]{2,1,0:T(8,128)}), f32[16,48,768]{2,1,0:T(8,128)S(1)}, u32[]{:S(2)}, u32[]{:S(2)}) async-start(f32[16,48,768]{2,1,0:T(8,128)} %stack.21), calls=%async_computation.1 | async-start | bytes 4718592 | tf_op jit(solution)/shard_map/all_to_all | solution.py:9
  715.7 62.3 %copy-start.9 = (f32[48,768]{1,0:T(8,128)S(1)}, f32[48,768]{1,0:T(8,128)}, u32[]{:S(2)}) copy-start(f32[48,768]{1,0:T(8,128)} %copy-done.8) | copy-start | bytes 442372
  748.7 38.6 %copy-start.7 = (f32[48,768]{1,0:T(8,128)S(1)}, f32[48,768]{1,0:T(8,128)}, u32[]{:S(2)}) copy-start(f32[48,768]{1,0:T(8,128)} %fusion.4) | copy-start | bytes 442372
  748.8 38.1 %collective-permute-start.2 = (f32[1,48,768]{2,1,0:T(8,128)S(1)}, f32[1,48,768]{2,1,0:T(8,128)S(1)}, u32[]{:S(2)}, u32[]{:S(2)}) collective-permute-start(f32[1,48,768]{2,1,0:T(8,128)S(1)} %convolution_bitcast_fusion.1), channel_id=1, source_target_pairs={{16,0},{32,16},{48,32},{64,48},{80,64},{96,80},{112,96},{128,112},... | collective-permute-start | bytes 442376 | tf_op jit(solution)/shard_map/ppermute | solution.py:25
  782.0 5.3 collective-permute-start.3
Sparse Core Ops, SparseCore 0:
  11.6 64.6 all-gather.11
  319.7 75.3 all-gather.5
  407.5 60.6 all-gather.7
  702.7 75.2 all-gather.9
